TPU v7x, 128 devices: a whole 4x4x4 slice. The times are simulated.
128 devices in a mesh: hid: 32 (over x_lo, z, y), dp: 4 (over x_hi, core).
Axes of the slice: x: 4 (x_hi: 2, x_lo: 2; x = x_hi * 2 + x_lo), y: 4, z: 4, core: 2. Of those that a mesh axis runs over, the one named last changes fastest.
Arguments:
- hidden_acts: bfloat16 [1024, 65536], P('dp', 'hid'), may hold values from -6 to 6
- out_grads: bfloat16 [1024, 1024], P('dp'), may hold values from -6 to 6
- damping: float32 [64], replicated, may hold values from 0.05 to 1
Outputs:
- update: bfloat16 [65536, 1024], P('hid')
All inputs are finite; a program needn't handle non-finite values.
Results may differ from a plain program's by a relative error of at most 0.0023.
Values may be sent and summed in bfloat16 or wider, within the bound.
A program may use at most 128 MiB of HBM per device.

v0:
```python
import jax
import jax.numpy as jnp
from jax import lax
from jax.sharding import PartitionSpec as P

BLOCK = 1024
ITERS = 3


out_damping = 0.1


def partner_2(value, axis, bit):
    mask = 2**bit
    pairs = [(source, source ^ mask) for source in range(lax.axis_size(axis))]
    return lax.ppermute(value, axis, pairs)


def join_block(local_rows):
    dp_place = lax.axis_index("dp")
    partner = partner_2(local_rows.astype(jnp.bfloat16), "dp", 0).astype(local_rows.dtype)
    upper = dp_place // 2**0 % 2 == 1
    local_rows = jnp.where(
        upper,
        jnp.concatenate([partner, local_rows], axis=1),
        jnp.concatenate([local_rows, partner], axis=1),
    )
    return local_rows


def spread_rows(local_rows):
    return lax.all_gather(local_rows, ("hid", "dp"), axis=1, tiled=True)


def identity_rows(first_row, row_count, width):
    row_ids = first_row + jnp.arange(row_count, dtype=jnp.int32)
    return (row_ids[:, None] == jnp.arange(width, dtype=jnp.int32)[None, :]).astype(jnp.float32)


def newton_rows(mat_rows, scales, first_row, complete):
    block_count, row_span, matrix_order = mat_rows.shape
    own_ident = identity_rows(first_row, row_span, matrix_order)
    scale_col = scales[:, None, None]
    local_rows = 2.0 * scale_col * own_ident[None] - scale_col * scale_col * mat_rows
    for iteration in range(1, ITERS):
        whole = complete(local_rows)
        product = jnp.einsum("nrk,nkc->nrc", mat_rows, whole, precision=lax.Precision.HIGHEST)
        product = jnp.einsum("nrk,nkc->nrc", product, whole, precision=lax.Precision.HIGHEST)
        own_rows = lax.dynamic_slice_in_dim(whole, first_row, row_span, 1)
        local_rows = 2.0 * own_rows - product
    return local_rows


def local(hidden_acts, out_grads, damping):
    tok_dev, hid_width = hidden_acts.shape
    width = out_grads.shape[1]
    dp_size = lax.axis_size("dp")
    hid_size = lax.axis_size("hid")
    dp_place = lax.axis_index("dp")
    hid_place = lax.axis_index("hid")
    row_count = hid_width // dp_size
    row_span = min(row_count, BLOCK)
    block_count = row_count // row_span
    blocks_hid = hid_width // BLOCK
    token_total = tok_dev * dp_size
    row_start = dp_place * row_count
    first_block = row_start // BLOCK
    offset = row_start % BLOCK
    s_count = width // (hid_size * dp_size)
    s_start = (hid_place * dp_size + dp_place) * s_count
    group_start = hid_place * (width // hid_size)
    group_count = width // hid_size
    local_blocks = hidden_acts.reshape(tok_dev, blocks_hid, BLOCK)
    gram_part = jnp.einsum(
        "tnb,tnc->nbc", local_blocks, local_blocks, preferred_element_type=jnp.float32
    ).reshape(hid_width, BLOCK)
    grad_part = jnp.einsum("tf,td->fd", hidden_acts, out_grads, preferred_element_type=jnp.float32)
    grad_group = lax.dynamic_slice_in_dim(out_grads, group_start, group_count, 1)
    s_part = jnp.einsum("tr,td->rd", grad_group, out_grads, preferred_element_type=jnp.float32)
    gram_rows, grad_rows, s_sum = (
        lax.psum_scatter(gram_part, "dp", scatter_dimension=0, tiled=True),
        lax.psum_scatter(grad_part, "dp", scatter_dimension=0, tiled=True),
        lax.psum_scatter(s_part, "dp", scatter_dimension=0, tiled=True),
    )
    block_damping = lax.dynamic_slice_in_dim(
        damping, hid_place * blocks_hid + first_block, block_count
    )
    in_rows = gram_rows.reshape(block_count, row_span, BLOCK) / token_total
    in_rows = in_rows + block_damping[:, None, None] * identity_rows(offset, row_span, BLOCK)[None]
    out_rows = s_sum / token_total + out_damping * identity_rows(s_start, s_count, width)
    block_ssq = jnp.sum(in_rows * in_rows, axis=(1, 2))
    ownership = (
        (first_block + jnp.arange(block_count, dtype=jnp.int32))[:, None]
        == jnp.arange(blocks_hid, dtype=jnp.int32)[None, :]
    ).astype(jnp.float32)
    block_norms = jnp.dot(block_ssq, ownership, precision=lax.Precision.HIGHEST)
    s_ssq = jnp.sum(out_rows * out_rows)
    norm_total, s_total = lax.psum((block_norms, s_ssq), "dp")
    s_total = lax.psum(s_total, "hid")
    block_scales = 1.0 / jnp.sqrt(jnp.dot(ownership, norm_total, precision=lax.Precision.HIGHEST))
    out_scale = (1.0 / jnp.sqrt(s_total)).reshape(1)
    out_local = newton_rows(out_rows[None], out_scale, s_start, spread_rows)
    out_inverse = spread_rows(out_local)[0]
    in_local = newton_rows(in_rows, block_scales, offset, join_block)
    right_rows = jnp.einsum(
        "nrd,de->nre",
        grad_rows.reshape(block_count, row_span, width),
        out_inverse,
        precision=lax.Precision.HIGHEST,
    )
    right_whole = join_block(right_rows)
    update_local = jnp.einsum(
        "nrk,nkd->nrd", in_local, right_whole, precision=lax.Precision.HIGHEST
    )
    update_local = update_local.reshape(row_count, width).astype(jnp.bfloat16)
    return lax.all_gather(update_local, "dp", axis=0, tiled=True)


def solution(mesh):
    return jax.shard_map(
        local,
        mesh=mesh,
        in_specs=(P("dp", "hid"), P("dp", None), P()),
        out_specs=P("hid", None),
        check_vma=False,
    )
```

profile of v0, /device:TPU:1, one launch (start us, length us, event | category | flops | bytes accessed | tf_op | source)
XLA Modules:
  0.0 980.1 jit_solution(1619043438353247402)
XLA Ops:
  6.5 1.0 copy-done
  7.6 0.9 fusion.40
  8.6 0.0 reduce-scatter.4.cloned.1.call-start
  8.6 6.1 fusion.35
  14.7 0.0 all-gather.11.cloned.1.call-start
  14.8 0.5 copy-done.8
  15.3 0.6 dynamic_slice.18
  16.0 23.1 %reduce-scatter.8.cloned.1.call-done = f32[8,1024]{1,0:T(8,128)} async-done(((f32[32,1024]{1,0:T(8,128)}), f32[8,1024]{1,0:T(8,128)}) %reduce-scatter.8.cloned.1.call-update) | async-done | bytes 32784 | tf_op jit(solution)/shard_map/reduce_scatter | solution.py:83
  39.1 1.5 multiply_reduce_fusion.1
  40.6 80.0 %reduce-scatter.4.cloned.1.call-done = f32[512,1024]{1,0:T(8,128)} async-done(((f32[2048,1024]{1,0:T(8,128)}), f32[512,1024]{1,0:T(8,128)}) %reduce-scatter.4.cloned.1.call-update) | async-done | bytes 2097168 | tf_op jit(solution)/shard_map/reduce_scatter | solution.py:81
  120.6 3.6 multiply_reduce_fusion
  124.2 0.7 compare_select_fusion.1
  124.9 7.8 all-reduce
  132.7 68.5 %psum.23 = f32[]{:T(128)} all-reduce(f32[]{:T(128)} %get-tuple-element.5), channel_id=1, replica_groups=mesh['hid'=32,'dp'=4] {'hid'}, use_global_device_ids=true, to_apply=%region_7.8 | all-reduce | flops 1 | bytes 8 | tf_op jit(solution)/shard_map/psum | solution.py:99
  201.9 0.7 multiply_subtract_fusion.1
  202.6 0.0 all-gather.11.cloned.1.call-update
  202.6 0.0 all-gather.13.cloned.1.call-start
  202.7 208.9 %all-gather.11.cloned.1.call-done = f32[1024,1024]{1,0:T(8,128)} async-done(((f32[8,1024]{1,0:T(8,128)}), f32[1024,1024]{1,0:T(8,128)}) %all-gather.11.cloned.1.call-update) | async-done | bytes 4194320 | tf_op jit(solution)/shard_map/all_gather | solution.py:32
  411.6 4.4 fusion.52
  416.0 2.7 convolution_subtract_fusion.1
  418.7 0.0 all-gather.13.cloned.1.call-update
  418.7 0.0 reduce-scatter.6.cloned.1.call-start
  418.8 4.5 fusion.54
  423.3 0.4 all-gather.7.cloned.1.call-start
  423.7 191.6 %all-gather.13.cloned.1.call-done = f32[1024,1024]{1,0:T(8,128)} async-done(((f32[8,1024]{1,0:T(8,128)}), f32[1024,1024]{1,0:T(8,128)}) %all-gather.13.cloned.1.call-update) | async-done | bytes 4194320 | tf_op jit(solution)/shard_map/all_gather | solution.py:32
  615.3 4.4 fusion.51
  619.7 2.7 fusion.34
  622.4 0.0 all-gather.9.cloned.1.call-start
  622.5 0.6 fusion.44
  623.8 3.0 convert_bitcast_fusion.1
  626.8 1.1 collective-permute-start
  628.0 3.5 collective-permute-done
  631.5 2.0 convert_bitcast_fusion.3
  633.5 7.8 fusion.11
  641.3 20.4 %fusion.53 = (bf16[1,512,1024]{2,1,0:T(8,128)(2,1)}, f32[1,512,1024]{2,1,0:T(8,128)}) fusion(f32[512,1024]{1,0:T(8,128)S(1)} %fusion.11, f32[512,1024]{1,0:T(8,128)S(1)} %copy-done.6, f32[512,1024]{1,0:T(8,128)S(1)} %get-tuple-element.11, pred[]{:T(512)S(6)} %eq.31, s32[]{:T(128)S(6)} %select_n.87, f32[1,512,1024]{2,1,0:T(8,128)S(1)} %get-tuple-element.12, ...), kind=kOutput, calls=%fused_computation.79 | convolution fusion | flops 6448742400 | bytes 13633024 | tf_op jit(solution)/shard_map/nrk,nkc->nrc/dot_general | solution.py:48
  661.7 0.2 collective-permute-start.1
  661.9 34.2 %reduce-scatter.6.cloned.1.call-done = f32[512,1024]{1,0:T(8,128)} async-done(((f32[2048,1024]{1,0:T(8,128)}), f32[512,1024]{1,0:T(8,128)}) %reduce-scatter.6.cloned.1.call-update) | async-done | bytes 2097168 | tf_op jit(solution)/shard_map/reduce_scatter | solution.py:82
  696.1 198.8 %all-gather.7.cloned.1.call-done = f32[1,1024,1024]{2,1,0:T(8,128)} async-done(((f32[1,8,1024]{2,1,0:T(8,128)}), f32[1,1024,1024]{2,1,0:T(8,128)}) %all-gather.7.cloned.1.call-update) | async-done | bytes 4194320 | tf_op jit(solution)/shard_map/all_gather | solution.py:32
  894.9 9.6 fusion.6
  904.5 0.2 convert_bitcast_fusion
  904.7 1.2 collective-permute-start.2
  905.9 1.7 convert_bitcast_fusion.2
  907.6 7.8 fusion.9
  915.5 6.9 fusion.8
  922.4 0.4 bitcast_convert_fusion
  922.8 8.5 fusion.31
  931.3 37.0 %all-gather.9.cloned.1.call-done = bf16[2048,1024]{1,0:T(8,128)(2,1)} async-done(((bf16[512,1024]{1,0:T(8,128)(2,1)}), bf16[2048,1024]{1,0:T(8,128)(2,1)}) %all-gather.9.cloned.1.call-update) | async-done | bytes 4194320 | tf_op jit(solution)/shard_map/all_gather | solution.py:116
  968.3 4.7 copy.14
  (28 shorter events, 0.1 us)
Async XLA Ops:
  6.5 1.0 copy-start
  6.5 32.6 %reduce-scatter.8.cloned.1.call-start = ((), (), s32[]{:S(2)}) async-start(), calls=%async_computation.5 | async-start | bytes 163840 | tf_op jit(solution)/shard_map/reduce_scatter | solution.py:83
  8.6 112.0 %reduce-scatter.4.cloned.1.call-start = ((), (), s32[]{:S(2)}) async-start(), calls=%async_computation.3 | async-start | bytes 10485760 | tf_op jit(solution)/shard_map/reduce_scatter | solution.py:81
  14.7 0.7 copy-start.8
  14.7 396.9 %all-gather.11.cloned.1.call-start = ((), (), s32[]{:S(2)}) async-start(), calls=%async_computation.8 | async-start | bytes 4227072 | tf_op jit(solution)/shard_map/all_gather | solution.py:32
  39.1 162.8 %copy-start.7 = (f32[8,1024]{1,0:T(8,128)S(1)}, f32[8,1024]{1,0:T(8,128)}, u32[]{:S(2)}) copy-start(f32[8,1024]{1,0:T(8,128)} %reduce-scatter.8.cloned.1.call-done) | copy-start | bytes 98308
  202.6 412.7 %all-gather.13.cloned.1.call-start = ((), (), s32[]{:S(2)}) async-start(), calls=%async_computation.9 | async-start | bytes 4227072 | tf_op jit(solution)/shard_map/all_gather | solution.py:32
  411.6 4.4 copy-start.3
  416.0 2.8 copy-start.5
  418.7 277.4 %reduce-scatter.6.cloned.1.call-start = ((), (), s32[]{:S(2)}) async-start(), calls=%async_computation.4 | async-start | bytes 10485760 | tf_op jit(solution)/shard_map/reduce_scatter | solution.py:82
  423.3 471.6 %all-gather.7.cloned.1.call-start = ((), (), s32[]{:S(2)}) async-start(), calls=%async_computation.6 | async-start | bytes 4227072 | tf_op jit(solution)/shard_map/all_gather | solution.py:32
  615.3 4.4 copy-start.2
  619.7 4.1 copy-start.4
  622.4 345.9 %all-gather.9.cloned.1.call-start = ((), (), s32[]{:S(2)}) async-start(), calls=%async_computation.7 | async-start | bytes 5242880 | tf_op jit(solution)/shard_map/all_gather | solution.py:116
  626.8 4.6 collective-permute-start
  628.0 5.5 copy-start.6
  661.7 244.2 %collective-permute-start.1 = (bf16[1,512,1024]{2,1,0:T(8,128)(2,1)}, bf16[1,512,1024]{2,1,0:T(8,128)(2,1)}, u32[]{:S(2)}, u32[]{:S(2)}) collective-permute-start(bf16[1,512,1024]{2,1,0:T(8,128)(2,1)} %get-tuple-element.13), channel_id=1, source_target_pairs={{0,1},{1,0},{2,3},{3,2},{4,5},{5,4},{6,7},{7,6},{8,9},{9,8},{10,11... | collective-permute-start | bytes 3145736 | tf_op jit(solution)/shard_map/ppermute | solution.py:16
  904.7 3.0 copy-start.9
  904.7 17.7 %collective-permute-start.2 = (bf16[1,512,1024]{2,1,0:T(8,128)(2,1)S(1)}, bf16[1,512,1024]{2,1,0:T(8,128)(2,1)S(1)}, u32[]{:S(2)}, u32[]{:S(2)}) collective-permute-start(bf16[1,512,1024]{2,1,0:T(8,128)(2,1)S(1)} %convert_bitcast_fusion), channel_id=1, source_target_pairs={{0,1},{1,0},{2,3},{3,2},{4,5},{5,4},{6,7},{7,6},{8,9},{9,8},{10,11... | collective-permute-start | bytes 3145736 | tf_op jit(solution)/shard_map/ppermute | solution.py:16
  968.3 4.7 copy-start.1
Sparse Core Ops, SparseCore 0:
  9.9 29.1 reduce-scatter.7
  42.0 78.5 reduce-scatter.3
  202.8 208.7 all-gather.10
  418.8 196.4 all-gather.12
  617.8 78.1 reduce-scatter.5
  697.8 197.0 all-gather.6
  931.5 36.7 all-gather.8
where the time goes:
time: 986 us; the launch traced here: 980 us
  waiting for transfers between devices  777 us (79%)
  matrix products  86.8 us (9%)
  blocking collectives  76.3 us (8%)
  between operations  15.3 us (2%)
  other arithmetic  14.4 us (1%)
    all_gather x3, waiting for transfers between devices, spread_rows(): return lax.all_gather(local_rows, ('hid', 'dp'), axis=1, tiled=True)  599 us
    reduce_scatter x1, waiting for transfers between devices, local(): lax.psum_scatter(gram_part, 'dp', scatter_dimension=0, tiled=True)  80 us
    psum x1, blocking collectives, local(): s_total = lax.psum(s_total, 'hid')  68.5 us
    all_gather x1, waiting for transfers between devices, local(): return lax.all_gather(update_local, 'dp', axis=0, tiled=True)  37 us
    reduce_scatter x1, waiting for transfers between devices, local(): lax.psum_scatter(grad_part, 'dp', scatter_dimension=0, tiled=True)  34.2 us
    dot_general x4, matrix products, newton_rows(): jnp.einsum('nrk,nkc->nrc', product, whole, precision=lax.Precision.HIGHEST)  32.6 us
    dot_general x4, matrix products, newton_rows(): jnp.einsum('nrk,nkc->nrc', mat_rows, whole, precision=lax.Precision.HIGHEST)  24.5 us
    reduce_scatter x1, waiting for transfers between devices, local(): lax.psum_scatter(s_part, 'dp', scatter_dimension=0, tiled=True)  23.1 us
  transfers between devices with their start and end apart: 10, of which 8 were waited for; matrix products, arithmetic and copies ran while one was open for 8% of the time, Pallas kernels for 0%

commit v1 on v0

v1 whole, which is shorter than its diff:
```python
import functools

import jax
import jax.numpy as jnp
from jax import lax
from jax.experimental import pallas as pl
from jax.experimental.pallas import tpu as pltpu
from jax.sharding import PartitionSpec as P

BLOCK = 1024
TILE = 512
OUT_DAMPING = 0.1
F32, BF16 = jnp.float32, jnp.bfloat16
MESH = pl.DeviceIdType.MESH
TOKENS_FIRST = (((0,), (0,)), ((), ()))

STAGE0, G_SIB, H_SIB, H_FAR, H_FARX = 0, 1, 2, 3, 4
STAGE1, STAGE2, FORWARD, CORR, RESULT = 5, 8, 11, 15, 17
OUT_TILES = 4
N_REMOTE = RESULT + OUT_TILES


def mm(a, b):
    return jnp.dot(a, b, preferred_element_type=F32)


def mmt(a, b):
    return lax.dot_general(a, b, TOKENS_FIRST, preferred_element_type=F32)


def tiles(count, size, body):
    def step(j, carry):
        body(j, pl.ds(pl.multiple_of(j * size, size), size))
        return carry

    lax.fori_loop(0, count, step, 0)


def kernel(h_hbm, g_hbm, damping, o_hbm, h, g, mo, mob, p2, p2b, p4b, cf, zb, zc,
           mi, y, ya, yb, part, send, recv, here):
    tok = h_hbm.shape[0]
    hid, dp = lax.axis_index("hid"), lax.axis_index("dp")
    xlo, zc_, yc_ = hid // 16, (hid // 4) % 4, hid % 4
    xhi, core = dp // 2, dp % 2

    first = yc_ + core * (zc_ - yc_)
    second = zc_ + core * (yc_ - zc_)

    def plane(move_first, move_second):
        f, s = (first + move_first) % 4, (second + move_second) % 4
        ny = f + core * (s - f)
        nz = s + core * (f - s)
        return (xlo * 16 + nz * 4 + ny, dp)

    sibling = (hid, xhi * 2 + 1 - core)
    far = (hid, (1 - xhi) * 2 + core)
    farx = (hid, (1 - xhi) * 2 + 1 - core)
    cut = ((1 - xlo) * 16 + zc_ * 4 + yc_, (1 - xhi) * 2 + core)
    firsts = [plane(i, 0) for i in range(1, 4)]
    seconds = [plane(0, i) for i in range(1, 4)]

    barrier = pltpu.get_barrier_semaphore()
    partners = [sibling, far, farx, cut] + firsts + seconds
    for partner in partners:
        pl.semaphore_signal(barrier, 1, device_id=partner, device_id_type=MESH)
    pl.semaphore_wait(barrier, len(partners))

    def remote(src, dst, slot, device):
        return pltpu.make_async_remote_copy(
            src_ref=src, dst_ref=dst, send_sem=send.at[slot], recv_sem=recv.at[slot],
            device_id=device, device_id_type=MESH)

    def slot(i):
        return pl.ds(i * tok, tok)

    def g_rows(base, start, size):
        return g.at[pl.ds(pl.multiple_of(base * tok + start, 16), size)]

    own_cols = pl.ds(pl.multiple_of(core * BLOCK, BLOCK), BLOCK)
    other_cols = pl.ds(pl.multiple_of((1 - core) * BLOCK, BLOCK), BLOCK)
    piece, group = tok // 16, tok // 4
    own_piece = (second * 4 + first) * piece

    stage0 = remote(g_hbm.at[pl.ds(pl.multiple_of(own_piece, 16), piece)],
                    g_rows(2, own_piece, piece), STAGE0, cut)
    stage0.start()
    g_own = pltpu.make_async_copy(g_hbm, g.at[slot(0)], here.at[0])
    g_own.start()
    g_sib = remote(g_hbm, g.at[slot(1)], G_SIB, sibling)
    g_sib.start()
    h_own = pltpu.make_async_copy(h_hbm.at[:, own_cols], h.at[slot(0)], here.at[1])
    h_own.start()
    h_sib = remote(h_hbm.at[:, other_cols], h.at[slot(1)], H_SIB, sibling)
    h_sib.start()
    h_far = remote(h_hbm.at[:, own_cols], h.at[slot(2)], H_FAR, far)
    h_far.start()
    h_farx = remote(h_hbm.at[:, other_cols], h.at[slot(3)], H_FARX, farx)
    h_farx.start()

    stage0.wait_recv()
    stage1 = [remote(g_rows(2, own_piece, piece), g_rows(2, own_piece, piece),
                     STAGE1 + i, firsts[i]) for i in range(3)]
    for copy in stage1:
        copy.start()

    g_own.wait()
    g_sib.wait_recv()

    def out_local(j, rs):
        mo[rs, :] = mmt(g[0:2 * tok, rs], g[0:2 * tok, :])

    tiles(2, TILE, out_local)

    for i in range(3):
        came = (second * 4 + (first + 3 - i) % 4) * piece
        remote(g_rows(2, came, piece), g_rows(2, came, piece), STAGE1 + i, firsts[i]).wait_recv()
    own_group = second * group
    stage2 = [remote(g_rows(2, own_group, group), g_rows(2, own_group, group),
                     STAGE2 + i, seconds[i]) for i in range(3)]
    for copy in stage2:
        copy.start()
    forwards = [remote(g_rows(2, own_group, group), g_rows(3, own_group, group), FORWARD, sibling)]
    forwards[0].start()

    h_own.wait()
    h_sib.wait_recv()

    def in_local(j, rs):
        mi[rs, :] = mmt(h[0:2 * tok, rs], h[0:2 * tok, :])
        y[rs, :] = mmt(h[0:2 * tok, rs], g[0:2 * tok, :])

    tiles(2, TILE, in_local)

    for i in range(3):
        came = ((second + 3 - i) % 4) * group
        remote(g_rows(2, came, group), g_rows(2, came, group), STAGE2 + i, seconds[i]).wait_recv()
        forward = remote(g_rows(2, came, group), g_rows(3, came, group), FORWARD + 1 + i, sibling)
        forward.start()
        forwards.append(forward)
    for i in range(4):
        came = ((first + 4 - i) % 4) * group
        remote(g_rows(3, came, group), g_rows(3, came, group), FORWARD + i, sibling).wait_recv()

    def ridge(j, size, amount):
        row = lax.broadcasted_iota(jnp.int32, (size, BLOCK), 0) + j * size
        col = lax.broadcasted_iota(jnp.int32, (size, BLOCK), 1)
        return jnp.where(row == col, amount, 0.0)

    def add_squares(j, m):
        squares = jnp.sum((m * m).reshape(TILE // 8, 8, BLOCK), axis=0)

        @pl.when(j == 0)
        def _():
            part[...] = squares

        @pl.when(j > 0)
        def _():
            part[...] += squares

    def scale():
        return 1.0 / jnp.sqrt(jnp.sum(part[...], keepdims=True))

    scale_tokens = 1.0 / (4 * tok)

    def out_factor(j, rs):
        m = mo[rs, :] + mmt(g[2 * tok:4 * tok, rs], g[2 * tok:4 * tok, :])
        m = m * scale_tokens + ridge(j, TILE, OUT_DAMPING)
        mo[rs, :] = m
        mob[rs, :] = m.astype(BF16)
        add_squares(j, m)

    tiles(2, TILE, out_factor)
    so = scale()

    def out_two(j, rs):
        n2 = (2.0 * so) * mo[rs, :] - (so * so) * mm(mob[rs, :], mob[...])
        p2[rs, :] = n2
        p2b[rs, :] = n2.astype(BF16)

    tiles(2, TILE, out_two)

    def mine(j):
        return pl.ds(pl.multiple_of(j * 2 * tok, tok), tok)

    def corr_one(j, rs):
        c1 = so * mm(g[mine(j), :], mob[...])
        cf[rs, :] = c1
        zb[rs, :] = (2.0 * g[mine(j), :].astype(F32) - c1).astype(BF16)

    tiles(2, tok, corr_one)

    def out_four(j, rs):
        n4 = 2.0 * p2[rs, :] - mm(p2b[rs, :], p2b[...])
        p4b[rs, :] = n4.astype(BF16)

    tiles(2, TILE, out_four)

    def corr_two(j, rs):
        c2 = 2.0 * cf[rs, :] + mm(zb[rs, :], p2b[...])
        cf[rs, :] = c2
        zb[rs, :] = (4.0 * g[mine(j), :].astype(F32) - c2).astype(BF16)

    tiles(2, tok, corr_two)

    def corr_three(j, rs):
        c3 = 2.0 * cf[rs, :] + mm(zb[rs, :], p4b[...])
        zc[mine(j), :] = (c3 * -0.125).astype(BF16)

    tiles(2, tok, corr_three)
    corr = [remote(zc.at[slot(2 * i)], zc.at[slot(2 * i + 1)], CORR + i, sibling) for i in range(2)]
    for copy in corr:
        copy.start()

    h_far.wait_recv()

    def in_far(j, rs):
        mi[rs, :] += mmt(h[2 * tok:3 * tok, rs], h[2 * tok:3 * tok, :])

    tiles(2, TILE, in_far)
    for copy in corr:
        copy.wait_recv()

    def right_far(j, rs):
        y[rs, :] += (mmt(h[2 * tok:3 * tok, rs], g[2 * tok:3 * tok, :])
                     + mmt(h[0:3 * tok, rs], zc[0:3 * tok, :]))

    tiles(2, TILE, right_far)

    h_farx.wait_recv()
    block_damping = damping[hid * 2 + core]

    def in_factor(j, rs):
        m = mi[rs, :] + mmt(h[3 * tok:4 * tok, rs], h[3 * tok:4 * tok, :])
        m = m * scale_tokens + ridge(j, TILE, block_damping)
        mi[rs, :] = m
        mob[rs, :] = m.astype(BF16)
        add_squares(j, m)

    tiles(2, TILE, in_factor)
    si = scale()

    def right_last(j, rs):
        r = (y[rs, :] + mmt(h[3 * tok:4 * tok, rs], g[3 * tok:4 * tok, :])
             + mmt(h[3 * tok:4 * tok, rs], zc[3 * tok:4 * tok, :]))
        y[rs, :] = r
        ya[rs, :] = r.astype(BF16)

    tiles(2, TILE, right_last)

    def in_two(j, rs):
        n2 = (2.0 * si) * mi[rs, :] - (si * si) * mm(mob[rs, :], mob[...])
        p2[rs, :] = n2
        p2b[rs, :] = n2.astype(BF16)

    tiles(2, TILE, in_two)

    def apply_one(j, rs):
        r = 2.0 * y[rs, :] - si * mm(mob[rs, :], ya[...])
        y[rs, :] = r
        yb[rs, :] = r.astype(BF16)

    tiles(2, TILE, apply_one)

    def in_four(j, rs):
        n4 = 2.0 * p2[rs, :] - mm(p2b[rs, :], p2b[...])
        p4b[rs, :] = n4.astype(BF16)

    tiles(2, TILE, in_four)

    def apply_two(j, rs):
        r = 2.0 * y[rs, :] - mm(p2b[rs, :], yb[...])
        y[rs, :] = r
        ya[rs, :] = r.astype(BF16)

    tiles(2, TILE, apply_two)

    final = 8.0 * si * so
    span = BLOCK // OUT_TILES

    def out_copies(j):
        src = yb.at[pl.ds(pl.multiple_of(j * span, span), span)]
        dst = o_hbm.at[pl.ds(pl.multiple_of(core * BLOCK + j * span, span), span)]
        return (pltpu.make_async_copy(src, dst, here.at[2 + j]),
                remote(src, dst, RESULT + j, sibling))

    def apply_three(j, rs):
        r = 2.0 * y[rs, :] - mm(p4b[rs, :], ya[...])
        yb[rs, :] = (final * r).astype(BF16)
        for copy in out_copies(j):
            copy.start()

    tiles(OUT_TILES, span, apply_three)

    for copy in [stage0, g_sib, h_sib, h_far, h_farx] + stage1 + stage2 + forwards + corr:
        copy.wait_send()
    for j in range(OUT_TILES):
        local_copy, far_copy = out_copies(j)
        local_copy.wait()
        far_copy.wait_send()
        src = yb.at[pl.ds(j * span, span)]
        dst = o_hbm.at[pl.ds(pl.multiple_of((1 - core) * BLOCK + j * span, span), span)]
        remote(src, dst, RESULT + j, sibling).wait_recv()


def local(hidden_acts, out_grads, damping):
    tok, width = hidden_acts.shape
    square = (BLOCK, BLOCK)
    hbm = pl.BlockSpec(memory_space=pl.ANY)
    return pl.pallas_call(
        kernel,
        name="kfac_step",
        out_shape=jax.ShapeDtypeStruct((width, BLOCK), BF16),
        in_specs=[hbm, hbm, pl.BlockSpec(memory_space=pltpu.SMEM)],
        out_specs=hbm,
        scratch_shapes=[
            pltpu.VMEM(square, BF16),
            pltpu.VMEM(square, BF16),
            pltpu.VMEM(square, F32),
            pltpu.VMEM(square, BF16),
            pltpu.VMEM(square, F32),
            pltpu.VMEM(square, BF16),
            pltpu.VMEM(square, BF16),
            pltpu.VMEM((BLOCK // 2, BLOCK), F32),
            pltpu.VMEM((BLOCK // 2, BLOCK), BF16),
            pltpu.VMEM(square, BF16),
            pltpu.VMEM(square, F32),
            pltpu.VMEM(square, F32),
            pltpu.VMEM(square, BF16),
            pltpu.VMEM(square, BF16),
            pltpu.VMEM((8, BLOCK), F32),
            pltpu.SemaphoreType.DMA((N_REMOTE,)),
            pltpu.SemaphoreType.DMA((N_REMOTE,)),
            pltpu.SemaphoreType.DMA((2 + OUT_TILES,)),
        ],
        compiler_params=pltpu.CompilerParams(
            collective_id=0, has_side_effects=True, vmem_limit_bytes=56 << 20
        ),
    )(hidden_acts, out_grads, damping)


def solution(mesh):
    return jax.shard_map(
        local,
        mesh=mesh,
        in_specs=(P("dp", "hid"), P("dp", None), P()),
        out_specs=P("hid", None),
        check_vma=False,
    )
```

time: 986 us -> 85.5 us (0.09)
  waiting for transfers between devices: 777 us -> 0 us
  matrix products: 86.8 us -> 0 us
  Pallas kernels: 0 us -> 80.7 us
  blocking collectives: 76.3 us -> 0 us
  between operations: 15.3 us -> 0.01 us
  other arithmetic: 14.4 us -> 0 us
    all_gather x4 -> x0, waiting for transfers between devices: 636 us -> none  [the longest x3 599 us: spread_rows(): return lax.all_gather(local_rows, ('hid', 'dp'), axis=1, tiled=True)]
    reduce_scatter x3 -> x0, waiting for transfers between devices: 137 us -> none  [the longest x1 80 us: local(): lax.psum_scatter(gram_part, 'dp', scatter_dimension=0, tiled=True)]
    dot_general x13 -> x0, matrix products: 86.8 us -> none  [the longest x4 32.6 us: newton_rows(): jnp.einsum('nrk,nkc->nrc', product, whole, precision=lax.Precision.HIGHEST)]
    pallas_call x0 -> x1, Pallas kernels: none -> 80.7 us  [local(): pl.pallas_call(kernel, name='kfac_step', out_shape=jax.ShapeDtypeStruct((...]
    psum x2 -> x0, blocking collectives: 76.3 us -> none  [the longest x1 68.5 us: local(): s_total = lax.psum(s_total, 'hid')]
  transfers between devices with their start and end apart: 10 -> 0, of which waited for: 8 -> 0; matrix products, arithmetic and copies ran while one was open for 8% -> 0% of each run, Pallas kernels for 0% -> 0%
where the time goes in v1:
time: 85.5 us; the launch traced here: 85.3 us
  Pallas kernels  80.7 us (94%)
  local copies, waits for them, and re-layouts  4.64 us (5%)
    pallas_call x1, Pallas kernels, local(): pl.pallas_call(kernel, name='kfac_step', out_shape=jax.ShapeDtypeStruct((...  80.7 us
    unnamed x1, local copies, waits for them, and re-layouts  4.64 us

profile of v1, /device:TPU:1, one launch (start us, length us, event | category | flops | bytes accessed | tf_op | source)
XLA Modules:
  0.0 85.3 jit_solution(8076605031792312798)
XLA Ops:
  0.0 80.7 %kfac_step.1 = bf16[2048,1024]{1,0:T(8,128)(2,1)} custom-call(bf16[256,2048]{1,0:T(8,128)(2,1)} %h_hbm.1, bf16[256,1024]{1,0:T(8,128)(2,1)} %g_hbm.1, f32[64]{0:T(128)} %damping.1), custom_call_target="tpu_custom_call" | custom-call | tf_op jit(solution)/shard_map/kfac_step/pallas_call | solution.py:309
  80.7 4.6 %copy.5 = bf16[2048,1024]{1,0:T(8,128)(2,1)} copy(bf16[2048,1024]{1,0:T(8,128)(2,1)} %kfac_step.1) | data formatting | bytes 8388608

commit v2 on v1

v2 whole, which is shorter than its diff:
```python
import jax
import jax.numpy as jnp
from jax import lax
from jax.experimental import pallas as pl
from jax.experimental.pallas import tpu as pltpu
from jax.sharding import PartitionSpec as P

BLOCK = 1024
OUT_DAMPING = 0.1
F32, BF16 = jnp.float32, jnp.bfloat16
MESH = pl.DeviceIdType.MESH
TOKENS_FIRST = (((0,), (0,)), ((), ()))

TOK = 256
GROUP = TOK // 4
PIECE = TOK // 16
PARTS = 8
PART = TOK // PARTS
ISSUE = (0, 0, 8, 8)
LATE = 3 * GROUP * 2
OUT_TILES = 4

STAGE0, G_SIB, H_SIB = 0, 1, 2
STAGE1, STAGE2, FORWARD, CORR = 3, 6, 9, 13
RESULT = 18
H_FAR = RESULT + OUT_TILES
H_FARX = H_FAR + PARTS
N_REMOTE = H_FARX + PARTS


def mm(a, b):
    return jnp.dot(a, b, preferred_element_type=F32)


def mmt(a, b):
    return lax.dot_general(a, b, TOKENS_FIRST, preferred_element_type=F32)


def total(m):
    rows = m.shape[0]
    return jnp.sum(jnp.sum((m * m).reshape(rows // 8, 8, BLOCK), axis=0), keepdims=True)


def ridge(amount):
    row = lax.broadcasted_iota(jnp.int32, (BLOCK, BLOCK), 0)
    col = lax.broadcasted_iota(jnp.int32, (BLOCK, BLOCK), 1)
    return jnp.where(row == col, amount, 0.0)


def step(body):
    body()


def kernel(h_hbm, g_hbm, damping, o_hbm, h, g, mo, mob, p2, p2b, p4b, cf, zb, zc,
           mi, y, ya, yb, send, recv, here):
    hid, dp = lax.axis_index("hid"), lax.axis_index("dp")
    xlo, zpos, ypos = hid // 16, (hid // 4) % 4, hid % 4
    xhi, core = dp // 2, dp % 2

    first = ypos + core * (zpos - ypos)
    second = zpos + core * (ypos - zpos)

    def plane(move_first, move_second):
        f, s = (first + move_first) % 4, (second + move_second) % 4
        ny = f + core * (s - f)
        nz = s + core * (f - s)
        return (xlo * 16 + nz * 4 + ny, dp)

    sibling = (hid, xhi * 2 + 1 - core)
    far = (hid, (1 - xhi) * 2 + core)
    farx = (hid, (1 - xhi) * 2 + 1 - core)
    cut = ((1 - xlo) * 16 + zpos * 4 + ypos, (1 - xhi) * 2 + core)
    firsts = [plane(i, 0) for i in range(1, 4)]
    seconds = [plane(0, i) for i in range(1, 4)]

    barrier = pltpu.get_barrier_semaphore()
    partners = [sibling, far, farx, cut] + firsts + seconds
    for partner in partners:
        pl.semaphore_signal(barrier, 1, device_id=partner, device_id_type=MESH)
    pl.semaphore_wait(barrier, len(partners))

    def remote(src, dst, slot, device):
        return pltpu.make_async_remote_copy(
            src_ref=src, dst_ref=dst, send_sem=send.at[slot], recv_sem=recv.at[slot],
            device_id=device, device_id_type=MESH)

    def far_row(side, group):
        return 2 * TOK + group * (2 * GROUP) + side * GROUP

    def g_piece(group, piece):
        return g.at[pl.ds(pl.multiple_of(far_row(0, group) + piece * PIECE, 16), PIECE)]

    def g_group(side, group):
        return g.at[pl.ds(pl.multiple_of(far_row(side, group), 16), GROUP)]

    own_cols = pl.ds(pl.multiple_of(core * BLOCK, BLOCK), BLOCK)
    other_cols = pl.ds(pl.multiple_of((1 - core) * BLOCK, BLOCK), BLOCK)

    h_sent = []

    def send_far(count):
        while len(h_sent) < 2 * count:
            part = len(h_sent) // 2
            rows = pl.ds(part * PART, PART)
            group, inside = part * PART // GROUP, part * PART % GROUP
            to_far = remote(h_hbm.at[rows, own_cols],
                            h.at[pl.ds(far_row(0, group) + inside, PART)], H_FAR + part, far)
            to_farx = remote(h_hbm.at[rows, other_cols],
                             h.at[pl.ds(far_row(1, group) + inside, PART)], H_FARX + part, farx)
            to_far.start()
            to_farx.start()
            h_sent.extend([to_far, to_farx])

    stage0 = remote(g_hbm.at[pl.ds(pl.multiple_of((second * 4 + first) * PIECE, 16), PIECE)],
                    g_piece(second, first), STAGE0, cut)
    stage0.start()
    g_own = pltpu.make_async_copy(g_hbm, g.at[pl.ds(0, TOK)], here.at[0])
    g_own.start()
    g_sib = remote(g_hbm, g.at[pl.ds(TOK, TOK)], G_SIB, sibling)
    g_sib.start()
    send_far(ISSUE[0])
    h_own = pltpu.make_async_copy(h_hbm.at[:, own_cols], h.at[pl.ds(0, TOK)], here.at[1])
    h_own.start()
    h_sib = remote(h_hbm.at[:, other_cols], h.at[pl.ds(TOK, TOK)], H_SIB, sibling)
    h_sib.start()

    stage0.wait_recv()
    stage1 = [remote(g_piece(second, first), g_piece(second, first), STAGE1 + i, firsts[i])
              for i in range(3)]
    for copy in stage1:
        copy.start()
    send_far(ISSUE[1])

    near = slice(0, 2 * TOK)
    rest = slice(2 * TOK, 4 * TOK)
    early = slice(2 * TOK, 2 * TOK + LATE)
    last = slice(2 * TOK + LATE, 4 * TOK)

    g_own.wait()
    g_sib.wait_recv()

    @step
    def out_local():
        mo[...] = mmt(g[near, :], g[near, :])

    for i in range(3):
        came = g_piece(second, (first + 3 - i) % 4)
        remote(came, came, STAGE1 + i, firsts[i]).wait_recv()
    stage2 = [remote(g_group(0, second), g_group(0, second), STAGE2 + i, seconds[i])
              for i in range(3)]
    for copy in stage2:
        copy.start()
    forwards = [remote(g_group(0, second), g_group(1, second), FORWARD, sibling)]
    forwards[0].start()
    send_far(ISSUE[2])

    h_own.wait()
    h_sib.wait_recv()

    @step
    def in_local():
        mi[...] = mmt(h[near, :], h[near, :])
        y[...] = mmt(h[near, :], g[near, :])

    for i in range(3):
        group = (second + 3 - i) % 4
        remote(g_group(0, group), g_group(0, group), STAGE2 + i, seconds[i]).wait_recv()
        forward = remote(g_group(0, group), g_group(1, group), FORWARD + 1 + i, sibling)
        forward.start()
        forwards.append(forward)
    send_far(ISSUE[3])
    for i in range(4):
        group = (first + 4 - i) % 4
        remote(g_group(1, group), g_group(1, group), FORWARD + i, sibling).wait_recv()

    scale_tokens = 1.0 / (4 * TOK)

    @step
    def out_factor():
        m = (mo[...] + mmt(g[rest, :], g[rest, :])) * scale_tokens + ridge(OUT_DAMPING)
        mo[...] = m
        mob[...] = m.astype(BF16)

    so = 1.0 / jnp.sqrt(total(mo[...]))

    mine = [(0, TOK)] + [(far_row(0, k), GROUP) for k in range(4)]

    def packed(ref):
        return jnp.concatenate([ref[a:a + n, :] for a, n in mine], axis=0)

    @step
    def out_two():
        n2 = (2.0 * so) * mo[...] - (so * so) * mm(mob[...], mob[...])
        p2[...] = n2
        p2b[...] = n2.astype(BF16)

    @step
    def corr_one():
        gm = packed(g)
        c1 = so * mm(gm, mob[...])
        cf[...] = c1
        zb[...] = (2.0 * gm.astype(F32) - c1).astype(BF16)

    @step
    def out_four():
        n4 = 2.0 * p2[...] - mm(p2b[...], p2b[...])
        p4b[...] = n4.astype(BF16)

    @step
    def corr_two():
        c2 = 2.0 * cf[...] + mm(zb[...], p2b[...])
        cf[...] = c2
        zb[...] = (4.0 * packed(g).astype(F32) - c2).astype(BF16)

    corr = []

    @step
    def corr_three():
        c3 = ((2.0 * cf[...] + mm(zb[...], p4b[...])) * -0.125).astype(BF16)
        at = 0
        for a, n in mine:
            zc[a:a + n, :] = c3[at:at + n, :]
            at += n

    for i, (a, n) in enumerate(mine):
        copy = remote(zc.at[pl.ds(a, n)], zc.at[pl.ds(a + n, n)], CORR + i, sibling)
        copy.start()
        corr.append(copy)

    def take_far(lo, hi):
        for part in range(lo, hi):
            h_sent[2 * part].wait_recv()
            h_sent[2 * part + 1].wait_recv()

    early_parts = LATE // (2 * PART)
    take_far(0, early_parts)

    @step
    def in_early():
        mi[...] += mmt(h[early, :], h[early, :])
        y[...] += mmt(h[early, :], g[early, :])

    for copy in corr:
        copy.wait_recv()

    @step
    def right_early():
        y[...] += mmt(h[0:2 * TOK + LATE, :], zc[0:2 * TOK + LATE, :])

    take_far(early_parts, PARTS)
    block_damping = damping[hid * 2 + core]

    @step
    def in_factor():
        m = (mi[...] + mmt(h[last, :], h[last, :])) * scale_tokens + ridge(block_damping)
        mi[...] = m
        mob[...] = m.astype(BF16)

    si = 1.0 / jnp.sqrt(total(mi[...]))

    @step
    def right_last():
        r = y[...] + mmt(h[last, :], g[last, :]) + mmt(h[last, :], zc[last, :])
        y[...] = r
        ya[...] = r.astype(BF16)

    @step
    def in_two():
        n2 = (2.0 * si) * mi[...] - (si * si) * mm(mob[...], mob[...])
        p2[...] = n2
        p2b[...] = n2.astype(BF16)

    @step
    def apply_one():
        r = 2.0 * y[...] - si * mm(mob[...], ya[...])
        y[...] = r
        yb[...] = r.astype(BF16)

    @step
    def in_four():
        n4 = 2.0 * p2[...] - mm(p2b[...], p2b[...])
        p4b[...] = n4.astype(BF16)

    @step
    def apply_two():
        r = 2.0 * y[...] - mm(p2b[...], yb[...])
        y[...] = r
        ya[...] = r.astype(BF16)

    final = 8.0 * si * so
    span = BLOCK // OUT_TILES

    def out_copies(j):
        src = yb.at[pl.ds(j * span, span)]
        dst = o_hbm.at[pl.ds(pl.multiple_of(core * BLOCK + j * span, span), span)]
        return (pltpu.make_async_copy(src, dst, here.at[2 + j]),
                remote(src, dst, RESULT + j, sibling))

    results = []
    for j in range(OUT_TILES):
        rs = slice(j * span, (j + 1) * span)

        @step
        def apply_three():
            r = 2.0 * y[rs, :] - mm(p4b[rs, :], ya[...])
            yb[rs, :] = (final * r).astype(BF16)

        copies = out_copies(j)
        for copy in copies:
            copy.start()
        results.append(copies)

    for copy in [stage0, g_sib, h_sib] + h_sent + stage1 + stage2 + forwards + corr:
        copy.wait_send()
    for j, (local_copy, far_copy) in enumerate(results):
        local_copy.wait()
        far_copy.wait_send()
        src = yb.at[pl.ds(j * span, span)]
        dst = o_hbm.at[pl.ds(pl.multiple_of((1 - core) * BLOCK + j * span, span), span)]
        remote(src, dst, RESULT + j, sibling).wait_recv()


def local(hidden_acts, out_grads, damping):
    width = hidden_acts.shape[1]
    square = (BLOCK, BLOCK)
    hbm = pl.BlockSpec(memory_space=pl.ANY)
    return pl.pallas_call(
        kernel,
        name="kfac_step",
        out_shape=jax.ShapeDtypeStruct((width, BLOCK), BF16),
        in_specs=[hbm, hbm, pl.BlockSpec(memory_space=pltpu.SMEM)],
        out_specs=hbm,
        scratch_shapes=[
            pltpu.VMEM(square, BF16),
            pltpu.VMEM(square, BF16),
            pltpu.VMEM(square, F32),
            pltpu.VMEM(square, BF16),
            pltpu.VMEM(square, F32),
            pltpu.VMEM(square, BF16),
            pltpu.VMEM(square, BF16),
            pltpu.VMEM((BLOCK // 2, BLOCK), F32),
            pltpu.VMEM((BLOCK // 2, BLOCK), BF16),
            pltpu.VMEM(square, BF16),
            pltpu.VMEM(square, F32),
            pltpu.VMEM(square, F32),
            pltpu.VMEM(square, BF16),
            pltpu.VMEM(square, BF16),
            pltpu.SemaphoreType.DMA((N_REMOTE,)),
            pltpu.SemaphoreType.DMA((N_REMOTE,)),
            pltpu.SemaphoreType.DMA((2 + OUT_TILES,)),
        ],
        compiler_params=pltpu.CompilerParams(
            collective_id=0, has_side_effects=True, vmem_limit_bytes=56 << 20
        ),
    )(hidden_acts, out_grads, damping)


def solution(mesh):
    return jax.shard_map(
        local,
        mesh=mesh,
        in_specs=(P("dp", "hid"), P("dp", None), P()),
        out_specs=P("hid", None),
        check_vma=False,
    )
```

time: 85.5 us -> 62.2 us (0.73)
  Pallas kernels: 80.7 us -> 57.4 us
    pallas_call x1, Pallas kernels: 80.7 us -> 57.4 us  [local(): pl.pallas_call(kernel, name='kfac_step', out_shape=jax.ShapeDtypeStruct((...]
where the time goes in v2:
time: 62.2 us; the launch traced here: 62 us
  Pallas kernels  57.4 us (92%)
  local copies, waits for them, and re-layouts  4.64 us (7%)
    pallas_call x1, Pallas kernels, local(): pl.pallas_call(kernel, name='kfac_step', out_shape=jax.ShapeDtypeStruct((...  57.4 us
    unnamed x1, local copies, waits for them, and re-layouts  4.64 us

profile of v2, /device:TPU:1, one launch (start us, length us, event | category | flops | bytes accessed | tf_op | source)
XLA Modules:
  0.0 62.0 jit_solution(12499234510864565016)
XLA Ops:
  0.0 57.4 %kfac_step.1 = bf16[2048,1024]{1,0:T(8,128)(2,1)} custom-call(bf16[256,2048]{1,0:T(8,128)(2,1)} %h_hbm.1, bf16[256,1024]{1,0:T(8,128)(2,1)} %g_hbm.1, f32[64]{0:T(128)} %damping.1), custom_call_target="tpu_custom_call" | custom-call | tf_op jit(solution)/shard_map/kfac_step/pallas_call | solution.py:327
  57.4 4.6 %copy.5 = bf16[2048,1024]{1,0:T(8,128)(2,1)} copy(bf16[2048,1024]{1,0:T(8,128)(2,1)} %kfac_step.1) | data formatting | bytes 8388608

commit v3 on v2

v3 whole, which is shorter than its diff:
```python
import jax
import jax.numpy as jnp
from jax import lax
from jax.experimental import pallas as pl
from jax.experimental.pallas import tpu as pltpu
from jax.sharding import PartitionSpec as P

BLOCK = 1024
OUT_DAMPING = 0.1
F32, BF16 = jnp.float32, jnp.bfloat16
MESH = pl.DeviceIdType.MESH
TOKENS_FIRST = (((0,), (0,)), ((), ()))

HALF = BLOCK // 2
TOP, LOW = slice(0, HALF), slice(HALF, BLOCK)

TOK = 256
GROUP = TOK // 4
START_PARTS = 0
PARTS = 8
PART = TOK // PARTS
LATE = 3 * GROUP * 2
OUT_TILES = 4

STAGE0, G_SIB, H_SIB, STAGE1, FORWARD, CORR, RESULT = 0, 1, 2, 3, 6, 10, 15
H_FAR = RESULT + OUT_TILES
H_FARX = H_FAR + PARTS
N_REMOTE = H_FARX + PARTS


def mm(a, b):
    return jnp.dot(a, b, preferred_element_type=F32)


def mmt(a, b):
    return lax.dot_general(a, b, TOKENS_FIRST, preferred_element_type=F32)


def total(m):
    rows, cols = m.shape
    return jnp.sum(jnp.sum((m * m).reshape(rows // 8, 8, cols), axis=0), keepdims=True)


def ridge(rows, cols, amount):
    row = lax.broadcasted_iota(jnp.int32, (rows, cols), 0)
    col = lax.broadcasted_iota(jnp.int32, (rows, cols), 1)
    return jnp.where(row == col, amount, 0.0)


def keep(ref, top, low):
    ref[TOP, :] = top
    ref[LOW, LOW] = low


def keep_whole(ref, top, low):
    keep(ref, top.astype(BF16), low.astype(BF16))
    ref[LOW, TOP] = top[:, LOW].astype(BF16).T


def gram(a):
    return mmt(a[:, TOP], a), mmt(a[:, LOW], a[:, LOW])


def add_gram(ref, a):
    top, low = gram(a)
    keep(ref, ref[TOP, :] + top, ref[LOW, LOW] + low)


def factor(ref, whole, a, scale, amount):
    top, low = gram(a)
    top = (ref[TOP, :] + top) * scale + ridge(HALF, BLOCK, amount)
    low = (ref[LOW, LOW] + low) * scale + ridge(HALF, HALF, amount)
    keep(ref, top, low)
    keep_whole(whole, top, low)
    return total(top[:, TOP]) + 2.0 * total(top[:, LOW]) + total(low)


def residual(ref, whole, linear, square):
    return (linear * ref[TOP, :] - square * mm(whole[TOP, :], whole[...]),
            linear * ref[LOW, LOW] - square * mm(whole[LOW, :], whole[:, LOW]))


def step(body):
    body()


def kernel(h_hbm, g_hbm, damping_hbm, u, h, g, mo, mob, p2, p2b, p4b, cf, zb, zc,
           mi, y, ya, yb, damping, send, recv, here):
    hid, dp = lax.axis_index("hid"), lax.axis_index("dp")
    xlo, zpos, ypos = hid // 16, (hid // 4) % 4, hid % 4
    xhi, core = dp // 2, dp % 2

    place = ypos + core * (zpos - ypos)

    def beside(move):
        ny = ypos + (1 - core) * ((ypos + move) % 4 - ypos)
        nz = zpos + core * ((zpos + move) % 4 - zpos)
        return (xlo * 16 + nz * 4 + ny, dp)

    sibling = (hid, xhi * 2 + 1 - core)
    far = (hid, (1 - xhi) * 2 + core)
    farx = (hid, (1 - xhi) * 2 + 1 - core)
    cut = ((1 - xlo) * 16 + zpos * 4 + ypos, (1 - xhi) * 2 + core)
    line = [beside(i) for i in range(1, 4)]

    own_cols = pl.ds(pl.multiple_of(core * BLOCK, BLOCK), BLOCK)
    other_cols = pl.ds(pl.multiple_of((1 - core) * BLOCK, BLOCK), BLOCK)
    g_own = pltpu.make_async_copy(g_hbm, g.at[pl.ds(0, TOK)], here.at[0])
    g_own.start()
    h_own = pltpu.make_async_copy(h_hbm.at[:, own_cols], h.at[pl.ds(0, TOK)], here.at[1])
    h_own.start()

    damping_own = pltpu.make_async_copy(damping_hbm, damping, here.at[2])
    damping_own.start()

    barrier = pltpu.get_barrier_semaphore()
    partners = [sibling, far, farx, cut] + line
    for partner in partners:
        pl.semaphore_signal(barrier, 1, device_id=partner, device_id_type=MESH)
    pl.semaphore_wait(barrier, len(partners))

    def remote(src, dst, slot, device):
        return pltpu.make_async_remote_copy(
            src_ref=src, dst_ref=dst, send_sem=send.at[slot], recv_sem=recv.at[slot],
            device_id=device, device_id_type=MESH)

    def far_row(side, group):
        return 2 * TOK + group * (2 * GROUP) + side * GROUP

    def g_group(side, group):
        return g.at[pl.ds(pl.multiple_of(far_row(side, group), 16), GROUP)]

    h_sent = []

    def send_far(count):
        while len(h_sent) < 2 * count:
            part = len(h_sent) // 2
            rows = pl.ds(part * PART, PART)
            group, inside = part * PART // GROUP, part * PART % GROUP
            to_far = remote(h_hbm.at[rows, own_cols],
                            h.at[pl.ds(far_row(0, group) + inside, PART)], H_FAR + part, far)
            to_farx = remote(h_hbm.at[rows, other_cols],
                             h.at[pl.ds(far_row(1, group) + inside, PART)], H_FARX + part, farx)
            to_far.start()
            to_farx.start()
            h_sent.extend([to_far, to_farx])

    stage0 = remote(g_hbm.at[pl.ds(pl.multiple_of(place * GROUP, GROUP), GROUP)],
                    g_group(0, place), STAGE0, cut)
    stage0.start()
    send_far(START_PARTS)
    g_sib = remote(g_hbm, g.at[pl.ds(TOK, TOK)], G_SIB, sibling)
    g_sib.start()
    h_sib = remote(h_hbm.at[:, other_cols], h.at[pl.ds(TOK, TOK)], H_SIB, sibling)
    h_sib.start()

    near = slice(0, 2 * TOK)
    rest = slice(2 * TOK, 4 * TOK)
    early = slice(2 * TOK, 2 * TOK + LATE)
    last = slice(2 * TOK + LATE, 4 * TOK)

    g_own.wait()
    g_sib.wait_recv()

    @step
    def out_local():
        keep(mo, *gram(g[near, :]))

    stage0.wait_recv()
    stage1 = [remote(g_group(0, place), g_group(0, place), STAGE1 + i, line[i]) for i in range(3)]
    for copy in stage1:
        copy.start()
    forwards = [remote(g_group(0, place), g_group(1, place), FORWARD, sibling)]
    forwards[0].start()
    send_far(PARTS)

    h_own.wait()
    h_sib.wait_recv()

    @step
    def in_local():
        keep(mi, *gram(h[near, :]))
        y[...] = mmt(h[near, :], g[near, :])

    for i in range(3):
        group = (place + 3 - i) % 4
        remote(g_group(0, group), g_group(0, group), STAGE1 + i, line[i]).wait_recv()
        forward = remote(g_group(0, group), g_group(1, group), FORWARD + 1 + i, sibling)
        forward.start()
        forwards.append(forward)
    sibling_place = zpos + core * (ypos - zpos)
    for i in range(4):
        group = (sibling_place + 4 - i) % 4
        remote(g_group(1, group), g_group(1, group), FORWARD + i, sibling).wait_recv()

    scale_tokens = 1.0 / (4 * TOK)

    so = 1.0 / jnp.sqrt(factor(mo, mob, g[rest, :], scale_tokens, OUT_DAMPING))

    mine = [(0, TOK)] + [(far_row(0, k), GROUP) for k in range(4)]

    def packed(ref):
        return jnp.concatenate([ref[a:a + n, :] for a, n in mine], axis=0)

    @step
    def out_two():
        two = residual(mo, mob, 2.0 * so, so * so)
        keep(p2, *two)
        keep_whole(p2b, *two)

    @step
    def corr_one():
        gm = packed(g)
        c1 = so * mm(gm, mob[...])
        cf[...] = c1
        zb[...] = (2.0 * gm.astype(F32) - c1).astype(BF16)

    @step
    def out_four():
        keep_whole(p4b, *residual(p2, p2b, 2.0, 1.0))

    @step
    def corr_two():
        c2 = 2.0 * cf[...] + mm(zb[...], p2b[...])
        cf[...] = c2
        zb[...] = (4.0 * packed(g).astype(F32) - c2).astype(BF16)

    corr = []

    @step
    def corr_three():
        c3 = ((2.0 * cf[...] + mm(zb[...], p4b[...])) * -0.125).astype(BF16)
        at = 0
        for a, n in mine:
            zc[a:a + n, :] = c3[at:at + n, :]
            at += n

    for i, (a, n) in enumerate(mine):
        copy = remote(zc.at[pl.ds(a, n)], zc.at[pl.ds(a + n, n)], CORR + i, sibling)
        copy.start()
        corr.append(copy)

    def take_far(lo, hi):
        for part in range(lo, hi):
            h_sent[2 * part].wait_recv()
            h_sent[2 * part + 1].wait_recv()

    early_parts = LATE // (2 * PART)
    take_far(0, early_parts)

    @step
    def in_early():
        add_gram(mi, h[early, :])
        y[...] += mmt(h[early, :], g[early, :])

    for copy in corr:
        copy.wait_recv()

    @step
    def right_early():
        y[...] += mmt(h[0:2 * TOK + LATE, :], zc[0:2 * TOK + LATE, :])

    take_far(early_parts, PARTS)
    damping_own.wait()
    block_damping = damping[hid * 2 + core]

    si = 1.0 / jnp.sqrt(factor(mi, mob, h[last, :], scale_tokens, block_damping))

    @step
    def right_last():
        r = y[...] + mmt(h[last, :], g[last, :]) + mmt(h[last, :], zc[last, :])
        y[...] = r
        ya[...] = r.astype(BF16)

    @step
    def in_two():
        two = residual(mi, mob, 2.0 * si, si * si)
        keep(p2, *two)
        keep_whole(p2b, *two)

    @step
    def apply_one():
        r = 2.0 * y[...] - si * mm(mob[...], ya[...])
        y[...] = r
        yb[...] = r.astype(BF16)

    @step
    def in_four():
        keep_whole(p4b, *residual(p2, p2b, 2.0, 1.0))

    @step
    def apply_two():
        r = 2.0 * y[...] - mm(p2b[...], yb[...])
        y[...] = r
        ya[...] = r.astype(BF16)

    final = 8.0 * si * so
    span = BLOCK // OUT_TILES

    def rows_of(owner, j):
        return u.at[pl.ds(pl.multiple_of(owner * BLOCK + j * span, span), span)]

    results = []
    for j in range(OUT_TILES):
        rs = slice(j * span, (j + 1) * span)

        @step
        def apply_three():
            r = 2.0 * y[rs, :] - mm(p4b[rs, :], ya[...])
            rows_of(core, j)[...] = (final * r).astype(BF16)

        results.append(remote(rows_of(core, j), rows_of(core, j), RESULT + j, sibling))
        results[j].start()

    for copy in [stage0, g_sib, h_sib] + h_sent + stage1 + forwards + corr + results:
        copy.wait_send()
    for j in range(OUT_TILES):
        remote(rows_of(1 - core, j), rows_of(1 - core, j), RESULT + j, sibling).wait_recv()


def local(hidden_acts, out_grads, damping):
    width = hidden_acts.shape[1]
    square = (BLOCK, BLOCK)
    hbm = pl.BlockSpec(memory_space=pl.ANY)
    return pl.pallas_call(
        kernel,
        name="kfac_step",
        out_shape=pltpu.VMEM((width, BLOCK), BF16),
        in_specs=[hbm, hbm, hbm],
        out_specs=pl.BlockSpec(memory_space=pltpu.VMEM),
        scratch_shapes=[
            pltpu.VMEM(square, BF16),
            pltpu.VMEM(square, BF16),
            pltpu.VMEM(square, F32),
            pltpu.VMEM(square, BF16),
            pltpu.VMEM(square, F32),
            pltpu.VMEM(square, BF16),
            pltpu.VMEM(square, BF16),
            pltpu.VMEM((BLOCK // 2, BLOCK), F32),
            pltpu.VMEM((BLOCK // 2, BLOCK), BF16),
            pltpu.VMEM(square, BF16),
            pltpu.VMEM(square, F32),
            pltpu.VMEM(square, F32),
            pltpu.VMEM(square, BF16),
            pltpu.VMEM(square, BF16),
            pltpu.SMEM((damping.shape[0],), F32),
            pltpu.SemaphoreType.DMA((N_REMOTE,)),
            pltpu.SemaphoreType.DMA((N_REMOTE,)),
            pltpu.SemaphoreType.DMA((3,)),
        ],
        compiler_params=pltpu.CompilerParams(
            collective_id=0, has_side_effects=True, vmem_limit_bytes=58 << 20
        ),
    )(hidden_acts, out_grads, damping)


def solution(mesh):
    return jax.shard_map(
        local,
        mesh=mesh,
        in_specs=(P("dp", "hid"), P("dp", None), P()),
        out_specs=P("hid", None),
        check_vma=False,
    )
```

time: 62.2 us -> 53.1 us (0.85)
  Pallas kernels: 57.4 us -> 51 us
  local copies, waits for them, and re-layouts: 4.64 us -> 2.02 us
    pallas_call x1, Pallas kernels: 57.4 us -> 51 us  [local(): pl.pallas_call(kernel, name='kfac_step', out_shape=pltpu.VMEM((width, BLO...]
    unnamed x1, local copies, waits for them, and re-layouts: 4.64 us -> 2.02 us
where the time goes in v3:
time: 53.1 us; the launch traced here: 53 us
  Pallas kernels  51 us (96%)
  local copies, waits for them, and re-layouts  2.02 us (4%)
    pallas_call x1, Pallas kernels, local(): pl.pallas_call(kernel, name='kfac_step', out_shape=pltpu.VMEM((width, BLO...  51 us
    unnamed x1, local copies, waits for them, and re-layouts  2.02 us

profile of v3, /device:TPU:1, one launch (start us, length us, event | category | flops | bytes accessed | tf_op | source)
XLA Modules:
  0.0 53.0 jit_solution(10920244724031527471)
XLA Ops:
  0.0 51.0 %kfac_step.1 = bf16[2048,1024]{1,0:T(8,128)(2,1)S(1)} custom-call(bf16[256,2048]{1,0:T(8,128)(2,1)} %h_hbm.1, bf16[256,1024]{1,0:T(8,128)(2,1)} %g_hbm.1, f32[64]{0:T(128)} %damping_hbm.1), custom_call_target="tpu_custom_call" | custom-call | tf_op jit(solution)/shard_map/kfac_step/pallas_call | solution.py:325
  51.0 2.0 %copy.5 = bf16[2048,1024]{1,0:T(8,128)(2,1)} copy(bf16[2048,1024]{1,0:T(8,128)(2,1)S(1)} %kfac_step.1) | data formatting | bytes 8388608

commit v4 on v3

--- a/solution.py
+++ b/solution.py
@@ -16,14 +16,13 @@
 
 TOK = 256
 GROUP = TOK // 4
-START_PARTS = 0
 PARTS = 8
 PART = TOK // PARTS
 LATE = 3 * GROUP * 2
-OUT_TILES = 4
+OUT_ROWS = (512, 256, 256)
 
 STAGE0, G_SIB, H_SIB, STAGE1, FORWARD, CORR, RESULT = 0, 1, 2, 3, 6, 10, 15
-H_FAR = RESULT + OUT_TILES
+H_FAR = RESULT + len(OUT_ROWS)
 H_FARX = H_FAR + PARTS
 N_REMOTE = H_FARX + PARTS
 
@@ -84,23 +83,21 @@
     body()
 
 
-def kernel(h_hbm, g_hbm, damping_hbm, u, h, g, mo, mob, p2, p2b, p4b, cf, zb, zc,
+def kernel(h_hbm, g_hbm, damping_hbm, u, h, ho, g, mo, mob, p2, p2b, p4b, cf, zb, zc,
            mi, y, ya, yb, damping, send, recv, here):
     hid, dp = lax.axis_index("hid"), lax.axis_index("dp")
     xlo, zpos, ypos = hid // 16, (hid // 4) % 4, hid % 4
     xhi, core = dp // 2, dp % 2
 
-    place = ypos + core * (zpos - ypos)
+    place = ypos
 
     def beside(move):
-        ny = ypos + (1 - core) * ((ypos + move) % 4 - ypos)
-        nz = zpos + core * ((zpos + move) % 4 - zpos)
-        return (xlo * 16 + nz * 4 + ny, dp)
+        ny = (ypos + move) % 4
+        return (xlo * 16 + zpos * 4 + ny, dp)
 
     sibling = (hid, xhi * 2 + 1 - core)
     far = (hid, (1 - xhi) * 2 + core)
     farx = (hid, (1 - xhi) * 2 + 1 - core)
-    cut = ((1 - xlo) * 16 + zpos * 4 + ypos, (1 - xhi) * 2 + core)
     line = [beside(i) for i in range(1, 4)]
 
     own_cols = pl.ds(pl.multiple_of(core * BLOCK, BLOCK), BLOCK)
@@ -110,11 +107,13 @@
     h_own = pltpu.make_async_copy(h_hbm.at[:, own_cols], h.at[pl.ds(0, TOK)], here.at[1])
     h_own.start()
 
+    h_other = pltpu.make_async_copy(h_hbm.at[:, other_cols], ho, here.at[3])
+    h_other.start()
     damping_own = pltpu.make_async_copy(damping_hbm, damping, here.at[2])
     damping_own.start()
 
     barrier = pltpu.get_barrier_semaphore()
-    partners = [sibling, far, farx, cut] + line
+    partners = [sibling, far, farx] + line
     for partner in partners:
         pl.semaphore_signal(barrier, 1, device_id=partner, device_id_type=MESH)
     pl.semaphore_wait(barrier, len(partners))
@@ -137,21 +136,23 @@
             part = len(h_sent) // 2
             rows = pl.ds(part * PART, PART)
             group, inside = part * PART // GROUP, part * PART % GROUP
-            to_far = remote(h_hbm.at[rows, own_cols],
+            to_far = remote(h.at[rows],
                             h.at[pl.ds(far_row(0, group) + inside, PART)], H_FAR + part, far)
-            to_farx = remote(h_hbm.at[rows, other_cols],
+            to_farx = remote(ho.at[rows],
                              h.at[pl.ds(far_row(1, group) + inside, PART)], H_FARX + part, farx)
             to_far.start()
             to_farx.start()
             h_sent.extend([to_far, to_farx])
 
     stage0 = remote(g_hbm.at[pl.ds(pl.multiple_of(place * GROUP, GROUP), GROUP)],
-                    g_group(0, place), STAGE0, cut)
+                    g_group(0, place), STAGE0, far)
     stage0.start()
-    send_far(START_PARTS)
+    h_own.wait()
+    h_other.wait()
+    send_far(PARTS)
     g_sib = remote(g_hbm, g.at[pl.ds(TOK, TOK)], G_SIB, sibling)
     g_sib.start()
-    h_sib = remote(h_hbm.at[:, other_cols], h.at[pl.ds(TOK, TOK)], H_SIB, sibling)
+    h_sib = remote(ho, h.at[pl.ds(TOK, TOK)], H_SIB, sibling)
     h_sib.start()
 
     near = slice(0, 2 * TOK)
@@ -172,9 +173,6 @@
         copy.start()
     forwards = [remote(g_group(0, place), g_group(1, place), FORWARD, sibling)]
     forwards[0].start()
-    send_far(PARTS)
-
-    h_own.wait()
     h_sib.wait_recv()
 
     @step
@@ -188,9 +186,8 @@
         forward = remote(g_group(0, group), g_group(1, group), FORWARD + 1 + i, sibling)
         forward.start()
         forwards.append(forward)
-    sibling_place = zpos + core * (ypos - zpos)
     for i in range(4):
-        group = (sibling_place + 4 - i) % 4
+        group = (place + 4 - i) % 4
         remote(g_group(1, group), g_group(1, group), FORWARD + i, sibling).wait_recv()
 
     scale_tokens = 1.0 / (4 * TOK)
@@ -295,27 +292,31 @@
         ya[...] = r.astype(BF16)
 
     final = 8.0 * si * so
-    span = BLOCK // OUT_TILES
-
-    def rows_of(owner, j):
-        return u.at[pl.ds(pl.multiple_of(owner * BLOCK + j * span, span), span)]
-
-    results = []
-    for j in range(OUT_TILES):
-        rs = slice(j * span, (j + 1) * span)
+
+    def rows_of(owner, start, size):
+        return u.at[pl.ds(pl.multiple_of(owner * BLOCK + start, 256), size)]
+
+    results, start = [], 0
+    for j, size in enumerate(OUT_ROWS):
+        rs = slice(start, start + size)
 
         @step
         def apply_three():
             r = 2.0 * y[rs, :] - mm(p4b[rs, :], ya[...])
-            rows_of(core, j)[...] = (final * r).astype(BF16)
-
-        results.append(remote(rows_of(core, j), rows_of(core, j), RESULT + j, sibling))
+            rows_of(core, start, size)[...] = (final * r).astype(BF16)
+
+        results.append(remote(rows_of(core, start, size), rows_of(core, start, size),
+                              RESULT + j, sibling))
         results[j].start()
+        start += size
 
     for copy in [stage0, g_sib, h_sib] + h_sent + stage1 + forwards + corr + results:
         copy.wait_send()
-    for j in range(OUT_TILES):
-        remote(rows_of(1 - core, j), rows_of(1 - core, j), RESULT + j, sibling).wait_recv()
+    start = 0
+    for j, size in enumerate(OUT_ROWS):
+        came = rows_of(1 - core, start, size)
+        remote(came, came, RESULT + j, sibling).wait_recv()
+        start += size
 
 
 def local(hidden_acts, out_grads, damping):
@@ -330,6 +331,7 @@
         out_specs=pl.BlockSpec(memory_space=pltpu.VMEM),
         scratch_shapes=[
             pltpu.VMEM(square, BF16),
+            pltpu.VMEM((TOK, BLOCK), BF16),
             pltpu.VMEM(square, BF16),
             pltpu.VMEM(square, F32),
             pltpu.VMEM(square, BF16),
@@ -346,7 +348,7 @@
             pltpu.SMEM((damping.shape[0],), F32),
             pltpu.SemaphoreType.DMA((N_REMOTE,)),
             pltpu.SemaphoreType.DMA((N_REMOTE,)),
-            pltpu.SemaphoreType.DMA((3,)),
+            pltpu.SemaphoreType.DMA((4,)),
         ],
         compiler_params=pltpu.CompilerParams(
             collective_id=0, has_side_effects=True, vmem_limit_bytes=58 << 20

time: 53.1 us -> 51.6 us (0.972)
  Pallas kernels: 51 us -> 49.5 us
    pallas_call x1, Pallas kernels: 51 us -> 49.5 us  [local(): pl.pallas_call(kernel, name='kfac_step', out_shape=pltpu.VMEM((width, BLO...]
where the time goes in v4:
time: 51.6 us; the launch traced here: 51.5 us
  Pallas kernels  49.5 us (96%)
  local copies, waits for them, and re-layouts  2.02 us (4%)
    pallas_call x1, Pallas kernels, local(): pl.pallas_call(kernel, name='kfac_step', out_shape=pltpu.VMEM((width, BLO...  49.5 us
    unnamed x1, local copies, waits for them, and re-layouts  2.02 us

profile of v4, /device:TPU:1, one launch (start us, length us, event | category | flops | bytes accessed | tf_op | source)
XLA Modules:
  0.0 51.5 jit_solution(14503111454184827662)
XLA Ops:
  0.0 49.5 %kfac_step.1 = bf16[2048,1024]{1,0:T(8,128)(2,1)S(1)} custom-call(bf16[256,2048]{1,0:T(8,128)(2,1)} %h_hbm.1, bf16[256,1024]{1,0:T(8,128)(2,1)} %g_hbm.1, f32[64]{0:T(128)} %damping_hbm.1), custom_call_target="tpu_custom_call" | custom-call | tf_op jit(solution)/shard_map/kfac_step/pallas_call | solution.py:326
  49.5 2.0 %copy.5 = bf16[2048,1024]{1,0:T(8,128)(2,1)} copy(bf16[2048,1024]{1,0:T(8,128)(2,1)S(1)} %kfac_step.1) | data formatting | bytes 8388608

commit v5 on v4

--- a/solution.py
+++ b/solution.py
@@ -19,7 +19,7 @@
 PARTS = 8
 PART = TOK // PARTS
 LATE = 3 * GROUP * 2
-OUT_ROWS = (512, 256, 256)
+OUT_ROWS = (512, 256, 128, 128)
 
 STAGE0, G_SIB, H_SIB, STAGE1, FORWARD, CORR, RESULT = 0, 1, 2, 3, 6, 10, 15
 H_FAR = RESULT + len(OUT_ROWS)
@@ -157,15 +157,9 @@
 
     near = slice(0, 2 * TOK)
     rest = slice(2 * TOK, 4 * TOK)
-    early = slice(2 * TOK, 2 * TOK + LATE)
+    half = slice(2 * TOK, 3 * TOK)
+    third = slice(3 * TOK, 2 * TOK + LATE)
     last = slice(2 * TOK + LATE, 4 * TOK)
-
-    g_own.wait()
-    g_sib.wait_recv()
-
-    @step
-    def out_local():
-        keep(mo, *gram(g[near, :]))
 
     stage0.wait_recv()
     stage1 = [remote(g_group(0, place), g_group(0, place), STAGE1 + i, line[i]) for i in range(3)]
@@ -173,6 +167,13 @@
         copy.start()
     forwards = [remote(g_group(0, place), g_group(1, place), FORWARD, sibling)]
     forwards[0].start()
+    g_own.wait()
+    g_sib.wait_recv()
+
+    @step
+    def out_local():
+        keep(mo, *gram(g[near, :]))
+
     h_sib.wait_recv()
 
     @step
@@ -224,6 +225,18 @@
 
     corr = []
 
+    def take_far(lo, hi):
+        for part in range(lo, hi):
+            h_sent[2 * part].wait_recv()
+            h_sent[2 * part + 1].wait_recv()
+
+    take_far(0, PARTS // 2)
+
+    @step
+    def in_half():
+        add_gram(mi, h[half, :])
+        y[...] += mmt(h[half, :], g[half, :])
+
     @step
     def corr_three():
         c3 = ((2.0 * cf[...] + mm(zb[...], p4b[...])) * -0.125).astype(BF16)
@@ -237,18 +250,13 @@
         copy.start()
         corr.append(copy)
 
-    def take_far(lo, hi):
-        for part in range(lo, hi):
-            h_sent[2 * part].wait_recv()
-            h_sent[2 * part + 1].wait_recv()
-
     early_parts = LATE // (2 * PART)
-    take_far(0, early_parts)
+    take_far(PARTS // 2, early_parts)
 
     @step
     def in_early():
-        add_gram(mi, h[early, :])
-        y[...] += mmt(h[early, :], g[early, :])
+        add_gram(mi, h[third, :])
+        y[...] += mmt(h[third, :], g[third, :])
 
     for copy in corr:
         copy.wait_recv()
@@ -294,7 +302,7 @@
     final = 8.0 * si * so
 
     def rows_of(owner, start, size):
-        return u.at[pl.ds(pl.multiple_of(owner * BLOCK + start, 256), size)]
+        return u.at[pl.ds(pl.multiple_of(owner * BLOCK + start, 128), size)]
 
     results, start = [], 0
     for j, size in enumerate(OUT_ROWS):

time: 51.6 us -> 51.5 us (level)
  no operation moved by 1% of the time
where the time goes in v5:
time: 51.5 us; the launch traced here: 51.4 us
  Pallas kernels  49.4 us (96%)
  local copies, waits for them, and re-layouts  2.02 us (4%)
    pallas_call x1, Pallas kernels, local(): pl.pallas_call(kernel, name='kfac_step', out_shape=pltpu.VMEM((width, BLO...  49.4 us
    unnamed x1, local copies, waits for them, and re-layouts  2.02 us

profile of v5, /device:TPU:1, one launch (start us, length us, event | category | flops | bytes accessed | tf_op | source)
XLA Modules:
  0.0 51.4 jit_solution(10561681090687322646)
XLA Ops:
  0.0 49.4 %kfac_step.1 = bf16[2048,1024]{1,0:T(8,128)(2,1)S(1)} custom-call(bf16[256,2048]{1,0:T(8,128)(2,1)} %h_hbm.1, bf16[256,1024]{1,0:T(8,128)(2,1)} %g_hbm.1, f32[64]{0:T(128)} %damping_hbm.1), custom_call_target="tpu_custom_call" | custom-call | tf_op jit(solution)/shard_map/kfac_step/pallas_call | solution.py:334
  49.4 2.0 %copy.5 = bf16[2048,1024]{1,0:T(8,128)(2,1)} copy(bf16[2048,1024]{1,0:T(8,128)(2,1)S(1)} %kfac_step.1) | data formatting | bytes 8388608
